TPU v7x, 256 devices: a whole 4x4x8 slice. The times are simulated.
256 devices in a mesh: wide: 128 (over y, z, x), cols: 2 (over core).
Axes of the slice: x: 4, y: 4, z: 8, core: 2. Of those that a mesh axis runs over, the one named last changes fastest.
Arguments:
- factor: float32 [262144, 256], P('wide', 'cols')
- gates: float32 [8, 128, 128], replicated, may hold values from -0.5 to 0.5
- gate_layout: int32 [2048], P('wide'), may hold values from 0 to 7
- jump_masks: int32 [3], replicated, may hold values from 1 to 127
- jump_rates: float32 [3], replicated, may hold values from 0.1 to 0.4
- sketch_perm: int32 [1024], replicated, may hold values from 0 to 1023, each once
- bases: float32 [8, 64, 64], replicated, may hold values from -0.75 to 0.75
- basis_index: int32 [128, 32], P('wide'), may hold values from 0 to 7
Outputs:
- new_factor: float32 [262144, 256], P('wide', 'cols')
- weights: float32 [128, 2048], P('wide', 'cols')
Inputs may be any that keep to these rules, and one draw needn't show every extreme that they name: `jump_masks`: nonzero bit masks over the high qubits. `sketch_perm`: each value appears once.
All inputs are finite; a program needn't handle non-finite values.
Results may differ from a plain program's by a relative error of at most 0.0003.
Values sent between devices are 32-bit elements; how exact they have to be, the bound alone decides.
No kernel may reach another device: no remote copies, remote signals or barrier semaphores. Data moves between devices by JAX's collectives and lax.ppermute only.
A program may use at most 64 MiB of HBM per device.

v0:
```python
import jax
import jax.numpy as jnp
from jax import lax
from jax.sharding import PartitionSpec as P

NS_ITERS = 7
HIGH = lax.Precision.HIGHEST


def apply_blocks(mats, index, data):
    chosen = jnp.take(mats, index, axis=0)
    return jnp.einsum("bij,bjc->bic", chosen, data, precision=HIGH)


def flip_rows(data, mask, count):
    shaped = data.reshape(count, data.shape[0] // count, data.shape[1])
    source = jnp.bitwise_xor(jnp.arange(count, dtype=jnp.int32), mask)
    return jnp.take(shaped, source, axis=0).reshape(data.shape)


def sketch_table(sketch_perm, rank):
    target = sketch_perm % rank
    sign = 1.0 - 2.0 * (sketch_perm // rank % 2).astype(jnp.float32)
    hit = target[:, None] == jnp.arange(rank, dtype=jnp.int32)[None, :]
    return jnp.where(hit, sign[:, None], jnp.zeros((), jnp.float32))


def mixed_stack(source, table, first, coefs, masks, count):
    rank = table.shape[1]
    width = source.shape[1]
    sources = []
    blocks = []
    for k in range(len(coefs)):
        flipped = source if k == 0 else flip_rows(source, masks[k - 1], count)
        sources.append(coefs[k] * flipped)
        blocks.append(lax.dynamic_slice_in_dim(table, k * rank + first, width, 0))
    joined = jnp.concatenate(sources, axis=1)
    table_rows = jnp.concatenate(blocks, axis=0)
    return jnp.dot(joined, table_rows, precision=HIGH, preferred_element_type=jnp.float32)


def newton_root(mat, eye, iters):
    fro = jnp.sqrt(jnp.sum(mat * mat))
    approx = mat / (fro + 1e-06)
    inverse = eye
    for step in range(iters):
        middle = 1.5 * eye - 0.5 * jnp.dot(inverse, approx, precision=HIGH)
        approx = jnp.dot(approx, middle, precision=HIGH)
        inverse = jnp.dot(middle, inverse, precision=HIGH)
    return (approx, inverse, fro)


def per_device(factor, gates, gate_layout, jump_masks, jump_rates, sketch_perm, bases, basis_index):
    rows, width = factor.shape
    order = gates.shape[1]
    count = lax.axis_size("wide")
    halves = lax.axis_size("cols")
    column_index = lax.axis_index("cols")
    rank = width * halves
    jumps = jump_rates.shape[0]
    gated = apply_blocks(gates, gate_layout, factor.reshape(rows // order, order, width)).reshape(
        rows, width
    )
    moved = lax.all_to_all(gated, "wide", split_axis=0, concat_axis=0, tiled=True)
    keep = 1.0 - 0.5 * jnp.sum(jump_rates)
    coefs = [keep] + [jnp.sqrt(jump_rates[k]) for k in range(jumps)]
    table = sketch_table(sketch_perm, rank)
    first = column_index * width
    terms = mixed_stack(moved, table, first, coefs, jump_masks, count)
    sketch_own = lax.psum_scatter(terms, "cols", scatter_dimension=1, tiled=True)
    sketch = lax.all_gather(sketch_own, "cols", axis=1, tiled=True)
    share = rows // halves
    mine = lax.dynamic_slice_in_dim(sketch, column_index * share, share, 0)
    gram_part = lax.dot_general(
        mine, mine, (((0,), (0,)), ((), ())), precision=HIGH, preferred_element_type=jnp.float32
    )
    gram = lax.psum(gram_part, ("wide", "cols"))
    eye = jnp.eye(rank, dtype=jnp.float32)
    unused, inverse, fro = newton_root(gram, eye, NS_ITERS)
    parts = []
    for k in range(jumps + 1):
        right = moved if k == 0 else flip_rows(moved, jump_masks[k - 1], count)
        parts.append(
            coefs[k]
            * lax.dot_general(
                sketch,
                right,
                (((0,), (0,)), ((), ())),
                precision=HIGH,
                preferred_element_type=jnp.float32,
            )
        )
    proj_own = jnp.concatenate(parts, axis=1)
    proj_sum = lax.psum(proj_own, "wide")
    coeff = lax.dot_general(
        inverse,
        proj_sum,
        (((0,), (0,)), ((), ())),
        precision=HIGH,
        preferred_element_type=jnp.float32,
    )
    core_part = lax.dot_general(
        coeff, coeff, (((1,), (1,)), ((), ())), precision=HIGH, preferred_element_type=jnp.float32
    )
    core = lax.psum(core_part, "cols")
    approx_two, unused_two, fro_two = newton_root(core, eye, NS_ITERS)
    root_own = jnp.sqrt(fro_two + 1e-06) * lax.dynamic_slice_in_dim(approx_two, first, width, 1)
    mixing_own = jnp.dot(inverse, root_own, precision=HIGH)
    new_own = jnp.dot(sketch, mixing_own, precision=HIGH)
    rot = bases.shape[1]
    rotated = apply_blocks(bases, basis_index.reshape(-1), new_own.reshape(rows // rot, rot, width))
    partial_value = (jnp.sum(rotated * rotated, axis=2) / rank).reshape(1, rows)
    weights = lax.psum_scatter(partial_value, "cols", scatter_dimension=1, tiled=True)
    return (new_own, weights)


def solution(mesh):
    return jax.shard_map(
        per_device,
        mesh=mesh,
        in_specs=(P("wide", "cols"), P(), P("wide"), P(), P(), P(), P(), P("wide", None)),
        out_specs=(P("wide", "cols"), P("wide", "cols")),
        check_vma=False,
    )
```

profile of v0, /device:TPU:1, one launch (start us, length us, event | category | flops | bytes accessed | tf_op | source)
XLA Modules:
  0.0 657.7 jit_solution(18310592391966807667)
XLA Ops:
  7.2 0.7 compare_select_fusion.5
  7.9 0.7 compare_and_fusion.4
  8.6 1.7 gather_fusion
  10.3 2.2 fusion.12
  12.5 16.3 %all-to-all-start = ((f32[128,16,128]{2,1,0:T(8,128)}), f32[128,16,128]{2,1,0:T(8,128)S(1)}, u32[]{:S(2)}, u32[]{:S(2)}) async-start(f32[128,16,128]{2,1,0:T(8,128)} %bitcast.1), calls=%async_computation | async-start | bytes 2097152 | tf_op jit(solution)/shard_map/all_to_all | solution.py:64
  28.9 0.7 fusion.47
  31.7 0.6 reduce_sum.36
  32.9 0.7 fusion.46
  33.6 0.6 compare_select_fusion.2
  34.3 1.2 compare_and_fusion.2
  35.5 1.3 compare_select_fusion
  36.7 1.8 compare_and_fusion
  38.9 0.7 constant_dynamic-slice_fusion.3
  39.6 16.5 %all-to-all-done = f32[128,16,128]{2,1,0:T(8,128)S(1)} async-done(((f32[128,16,128]{2,1,0:T(8,128)}), f32[128,16,128]{2,1,0:T(8,128)S(1)}, u32[]{:S(2)}, u32[]{:S(2)}) %all-to-all-start) | async-done | bytes 1048608 | tf_op jit(solution)/shard_map/all_to_all | solution.py:64
  56.1 0.8 gather_fusion.3
  56.8 0.9 broadcast_select_fusion.1
  57.7 1.0 copy-done.4
  58.7 1.0 broadcast_multiply_fusion.1
  59.7 0.8 gather_fusion.4
  60.7 1.0 copy-done.5
  61.7 1.0 broadcast_multiply_fusion
  62.7 0.8 gather_fusion.2
  63.9 0.8 copy-done.7
  64.7 0.6 copy-done.12
  65.7 4.9 fusion
  70.6 13.1 %reduce-scatter.5.cloned.1.call-done = f32[2048,128]{1,0:T(8,128)} async-done(((f32[2048,256]{1,0:T(8,128)}), f32[2048,128]{1,0:T(8,128)}) %reduce-scatter.5.cloned.1.call-update) | async-done | bytes 1048592 | tf_op jit(solution)/shard_map/reduce_scatter | solution.py:70
  83.8 19.0 %all-gather.2.cloned.1.call-done = f32[2048,256]{1,0:T(8,128)} async-done(((f32[2048,128]{1,0:T(8,128)}), f32[2048,256]{1,0:T(8,128)}) %all-gather.2.cloned.1.call-update) | async-done | bytes 2097168 | tf_op jit(solution)/shard_map/all_gather | solution.py:71
  102.7 4.1 fusion.10
  106.9 0.5 all-reduce.6.cloned.1.call-start
  107.4 5.4 convolution_multiply_fusion.16
  112.8 3.4 convolution_multiply_fusion.15
  116.3 3.4 convolution_multiply_fusion.17
  119.7 3.6 convolution_multiply_fusion.18
  123.3 0.8 pad_maximum_fusion
  124.2 234.4 %all-reduce.4.cloned.1.call-done = f32[256,256]{1,0:T(8,128)} async-done(((f32[256,256]{1,0:T(8,128)}), f32[256,256]{1,0:T(8,128)}) %all-reduce.4.cloned.1.call-update) | async-done | bytes 262160 | tf_op jit(solution)/shard_map/psum | solution.py:77
  358.6 1.6 multiply_reduce_fusion.1
  360.9 1.3 select_subtract_fusion.13
  362.5 1.3 fusion.31
  363.8 0.4 select_subtract_fusion.12
  365.0 0.4 select_subtract_fusion.11
  366.2 0.4 select_subtract_fusion.10
  367.3 0.4 select_subtract_fusion.9
  368.5 0.4 select_subtract_fusion.8
  369.7 0.4 select_subtract_fusion.7
  370.0 1.1 fusion.58
  371.1 206.0 %all-reduce.6.cloned.1.call-done = f32[256,512]{1,0:T(8,128)} async-done(((f32[256,512]{1,0:T(8,128)}), f32[256,512]{1,0:T(8,128)}) %all-reduce.6.cloned.1.call-update) | async-done | bytes 524304 | tf_op jit(solution)/shard_map/psum | solution.py:94
  577.2 1.7 fusion.59
  578.9 1.3 fusion.60
  580.6 1.6 gather_fusion.1
  582.2 30.0 %all-reduce.8.cloned.1.call-done = f32[256,256]{1,0:T(8,128)} async-done(((f32[256,256]{1,0:T(8,128)}), f32[256,256]{1,0:T(8,128)}) %all-reduce.8.cloned.1.call-update) | async-done | bytes 262160 | tf_op jit(solution)/shard_map/psum | solution.py:105
  612.2 1.6 multiply_reduce_fusion
  614.5 1.3 select_subtract_fusion.6
  616.0 1.3 fusion.32
  617.4 0.4 select_subtract_fusion.5
  622.0 0.4 select_subtract_fusion.1
  622.4 1.1 fusion.70
  623.9 1.3 select_subtract_fusion
  625.7 1.4 fusion.28
  627.1 1.8 fusion.72
  629.0 1.0 copy-done.9
  629.9 1.5 fusion.8
  631.5 2.0 div.43
  633.5 15.3 %reduce-scatter.7.cloned.1.call-done = f32[1024,1]{1,0:T(8,128)} async-done(((f32[2048,1]{1,0:T(8,128)}), f32[1024,1]{1,0:T(8,128)}) %reduce-scatter.7.cloned.1.call-update) | async-done | bytes 4112
  648.8 1.8 copy.11
  (85 shorter events, 11.1 us)
Async XLA Ops:
  7.2 3.1 copy-start
  10.3 18.6 %copy-start.16 = (f32[3]{0:T(128)S(1)}, f32[3]{0:T(128)}, u32[]{:S(2)}) copy-start(f32[3]{0:T(128)} %param.14) | copy-start | bytes 40
  10.3 22.6 %copy-start.17 = (s32[3]{0:T(128)S(1)}, s32[3]{0:T(128)}, u32[]{:S(2)}) copy-start(s32[3]{0:T(128)} %param.13) | copy-start | bytes 40
  10.3 28.2 %copy-start.15 = (s32[1024]{0:T(1024)S(1)}, s32[1024]{0:T(1024)}, u32[]{:S(2)}) copy-start(s32[1024]{0:T(1024)} %param.15) | copy-start | bytes 12292
  12.5 43.6 %all-to-all-start = ((f32[128,16,128]{2,1,0:T(8,128)}), f32[128,16,128]{2,1,0:T(8,128)S(1)}, u32[]{:S(2)}, u32[]{:S(2)}) async-start(f32[128,16,128]{2,1,0:T(8,128)} %bitcast.1), calls=%async_computation | async-start | bytes 2097152 | tf_op jit(solution)/shard_map/all_to_all | solution.py:64
  28.8 54.8 %reduce-scatter.5.cloned.1.call-start = ((), (), s32[]{:S(2)}) async-start(), calls=%async_computation.3 | async-start | bytes 3145728 | tf_op jit(solution)/shard_map/reduce_scatter | solution.py:70
  56.1 7.7 %copy-start.2 = (f32[128,16,128]{2,1,0:T(8,128)}, f32[128,16,128]{2,1,0:T(8,128)S(1)}, u32[]{:S(2)}) copy-start(f32[128,16,128]{2,1,0:T(8,128)S(1)} %all-to-all-done) | copy-start | bytes 3145732
  57.7 1.0 copy-start.4
  60.7 1.0 copy-start.5
  61.7 1.8 copy-start.18
  63.7 1.0 copy-start.7
  63.7 1.6 copy-start.12
  63.8 1.9 copy-start.13
  63.8 1.9 copy-start.14
  70.5 13.2 %copy-start.19 = (s32[1,32]{1,0:T(1,128)S(1)}, s32[1,32]{1,0:T(1,128)}, u32[]{:S(2)}) copy-start(s32[1,32]{1,0:T(1,128)} %param.17) | copy-start | bytes 388
  70.6 32.2 %all-gather.2.cloned.1.call-start = ((), (), s32[]{:S(2)}) async-start(), calls=%async_computation.4 | async-start | bytes 3145728 | tf_op jit(solution)/shard_map/all_gather | solution.py:71
  83.7 274.9 %all-reduce.4.cloned.1.call-start = ((), (), s32[]{:S(2)}) async-start(), calls=%async_computation.5 | async-start | bytes 524288 | tf_op jit(solution)/shard_map/psum | solution.py:77
  106.9 5.9 copy-start.1
  106.9 470.3 %all-reduce.6.cloned.1.call-start = ((), (), s32[]{:S(2)}) async-start(), calls=%async_computation.6 | async-start | bytes 1048576 | tf_op jit(solution)/shard_map/psum | solution.py:94
  107.4 5.4 copy-start.6
  112.8 3.5 copy-start.8
  116.3 3.5 copy-start.3
  124.2 488.0 %all-reduce.8.cloned.1.call-start = ((), (), s32[]{:S(2)}) async-start(), calls=%async_computation.7 | async-start | bytes 524288 | tf_op jit(solution)/shard_map/psum | solution.py:105
  369.6 210.9 %copy-start.11 = (f32[8,64,64]{2,1,0:T(8,128)S(1)}, f32[8,64,64]{2,1,0:T(8,128)}, u32[]{:S(2)}) copy-start(f32[8,64,64]{2,1,0:T(8,128)} %param.16) | copy-start | bytes 393220
  580.3 68.5 %reduce-scatter.7.cloned.1.call-start = ((), (), s32[]{:S(2)}) async-start(), calls=%async_computation.8 | async-start | bytes 1572864
  625.7 4.3 copy-start.10
  629.0 1.0 copy-start.9
Sparse Core Ops, SparseCore 0:
  70.7 12.9 reduce-scatter.4
  85.6 17.0 all-gather.1
  109.1 249.4 all-reduce.3
  365.3 211.7 all-reduce.5
  580.4 31.7 all-reduce.7
  633.6 15.1 reduce-scatter.6
where the time goes:
time: 666 us; the launch traced here: 658 us
  waiting for transfers between devices  534 us (80%)
  matrix products  55.9 us (8%)
  between operations  19.3 us (3%)
  starting transfers between devices  17.3 us (3%)
  local copies, waits for them, and re-layouts  16.1 us (2%)
  other arithmetic  14.9 us (2%)
    psum x1, waiting for transfers between devices, per_device(): gram = lax.psum(gram_part, ('wide', 'cols'))  234 us
    psum x1, waiting for transfers between devices, per_device(): proj_sum = lax.psum(proj_own, 'wide')  206 us
    psum x1, waiting for transfers between devices, per_device(): core = lax.psum(core_part, 'cols')  30 us
    all_gather x1, waiting for transfers between devices, per_device(): sketch = lax.all_gather(sketch_own, 'cols', axis=1, tiled=True)  19 us
    all_to_all x1, waiting for transfers between devices, per_device(): lax.all_to_all(gated, 'wide', split_axis=0, concat_axis=0, tiled=True)  16.5 us
    all_to_all x1, starting transfers between devices, per_device(): lax.all_to_all(gated, 'wide', split_axis=0, concat_axis=0, tiled=True)  16.3 us
    dot_general x4, matrix products, per_device(): lax.dot_general(sketch, right, (((0,), (0,)), ((), ())), precision=HIGH,...  15.9 us
    unnamed x7, waiting for transfers between devices  15.4 us
  transfers between devices with their start and end apart: 7, of which 7 were waited for; matrix products, arithmetic and copies ran while one was open for 6% of the time, Pallas kernels for 0%

commit v1 on v0

--- a/solution.py
+++ b/solution.py
@@ -74,7 +74,7 @@
     gram_part = lax.dot_general(
         mine, mine, (((0,), (0,)), ((), ())), precision=HIGH, preferred_element_type=jnp.float32
     )
-    gram = lax.psum(gram_part, ("wide", "cols"))
+    gram = lax.psum(lax.psum(gram_part, "cols"), "wide")
     eye = jnp.eye(rank, dtype=jnp.float32)
     unused, inverse, fro = newton_root(gram, eye, NS_ITERS)
     parts = []

time: 666 us -> 459 us (0.69)
  waiting for transfers between devices: 534 us -> 328 us
    psum x2, waiting for transfers between devices: 440 us -> 234 us  [per_device(): gram = lax.psum(lax.psum(gram_part, 'cols'), 'wide')]
where the time goes in v1:
time: 459 us; the launch traced here: 450 us
  waiting for transfers between devices  328 us (71%)
  matrix products  54 us (12%)
  between operations  19.2 us (4%)
  starting transfers between devices  17.3 us (4%)
  local copies, waits for them, and re-layouts  16.8 us (4%)
  other arithmetic  14.8 us (3%)
    psum x2, waiting for transfers between devices, per_device(): gram = lax.psum(lax.psum(gram_part, 'cols'), 'wide')  234 us
    psum x1, waiting for transfers between devices, per_device(): core = lax.psum(core_part, 'cols')  29.8 us
    all_gather x1, waiting for transfers between devices, per_device(): sketch = lax.all_gather(sketch_own, 'cols', axis=1, tiled=True)  19 us
    all_to_all x1, waiting for transfers between devices, per_device(): lax.all_to_all(gated, 'wide', split_axis=0, concat_axis=0, tiled=True)  16.6 us
    all_to_all x1, starting transfers between devices, per_device(): lax.all_to_all(gated, 'wide', split_axis=0, concat_axis=0, tiled=True)  16.3 us
    dot_general x4, matrix products, per_device(): lax.dot_general(sketch, right, (((0,), (0,)), ((), ())), precision=HIGH,...  15.9 us
    unnamed x7, waiting for transfers between devices  15.4 us
    reduce_scatter x1, waiting for transfers between devices, per_device(): lax.psum_scatter(terms, 'cols', scatter_dimension=1, tiled=True)  13.1 us
  transfers between devices with their start and end apart: 7, of which 7 were waited for; matrix products, arithmetic and copies ran while one was open for 6% of the time, Pallas kernels for 0%

profile of v1, /device:TPU:1, one launch (start us, length us, event | category | flops | bytes accessed | tf_op | source)
XLA Modules:
  0.0 450.5 jit_solution(9941971261360289511)
XLA Ops:
  7.2 0.7 compare_select_fusion.5
  7.9 0.7 compare_and_fusion.4
  8.6 1.7 gather_fusion
  10.3 2.2 fusion.12
  12.5 16.3 %all-to-all-start = ((f32[128,16,128]{2,1,0:T(8,128)}), f32[128,16,128]{2,1,0:T(8,128)S(1)}, u32[]{:S(2)}, u32[]{:S(2)}) async-start(f32[128,16,128]{2,1,0:T(8,128)} %bitcast.1), calls=%async_computation | async-start | bytes 2097152 | tf_op jit(solution)/shard_map/all_to_all | solution.py:64
  28.9 0.6 fusion.47
  31.6 0.6 reduce_sum.36
  32.8 0.6 fusion.46
  33.5 0.6 compare_select_fusion.2
  34.1 1.2 compare_and_fusion.2
  35.3 1.2 compare_select_fusion
  36.6 1.8 compare_and_fusion
  38.8 0.7 constant_dynamic-slice_fusion.3
  39.5 16.6 %all-to-all-done = f32[128,16,128]{2,1,0:T(8,128)S(1)} async-done(((f32[128,16,128]{2,1,0:T(8,128)}), f32[128,16,128]{2,1,0:T(8,128)S(1)}, u32[]{:S(2)}, u32[]{:S(2)}) %all-to-all-start) | async-done | bytes 1048608 | tf_op jit(solution)/shard_map/all_to_all | solution.py:64
  56.1 0.8 gather_fusion.3
  56.8 0.9 broadcast_select_fusion.1
  57.7 1.0 copy-done.3
  58.7 1.1 broadcast_multiply_fusion.1
  59.7 0.8 gather_fusion.4
  60.7 1.0 copy-done.5
  61.7 1.0 broadcast_multiply_fusion
  62.7 0.8 gather_fusion.2
  63.9 0.8 copy-done.7
  64.7 0.6 copy-done.13
  65.7 4.9 %fusion = f32[2048,256]{1,0:T(8,128)} fusion(f32[2048,128]{1,0:T(8,128)S(1)} %copy-done.14, f32[2048,128]{1,0:T(8,128)S(1)} %copy-done.13, f32[2048,128]{1,0:T(8,128)S(1)} %get-tuple-element.19, f32[2048,128]{1,0:T(8,128)S(1)} %get-tuple-element.20, f32[128,256]{1,0:T(8,128)S(1)} %get-tuple-element.6, f32[128,256]{1,0:T(8,128)S(1)} %get-tuple-element.7, ...), kind=kOutput, calls=%fused_computation.5 | convolution fusion | flops 3224764416 | bytes 6815744 | tf_op jit(solution)/shard_map/dot_general | solution.py:39
  70.6 13.1 %reduce-scatter.5.cloned.1.call-done = f32[2048,128]{1,0:T(8,128)} async-done(((f32[2048,256]{1,0:T(8,128)}), f32[2048,128]{1,0:T(8,128)}) %reduce-scatter.5.cloned.1.call-update) | async-done | bytes 1048592 | tf_op jit(solution)/shard_map/reduce_scatter | solution.py:70
  83.7 19.0 %all-gather.2.cloned.1.call-done = f32[2048,256]{1,0:T(8,128)} async-done(((f32[2048,128]{1,0:T(8,128)}), f32[2048,256]{1,0:T(8,128)}) %all-gather.2.cloned.1.call-update) | async-done | bytes 2097168 | tf_op jit(solution)/shard_map/all_gather | solution.py:71
  102.7 4.1 fusion.10
  106.8 0.5 all-reduce.9.cloned.1.call-start
  107.4 5.4 %convolution_multiply_fusion.18 = f32[256,128]{1,0:T(8,128)S(1)} fusion(f32[2048,256]{1,0:T(8,128)} %all-gather.2.cloned.1.call-done, f32[2048,128]{1,0:T(8,128)} %bitcast.115, f32[]{:T(128)S(6)} %sub.57), kind=kOutput, calls=%fused_computation.46 | convolution fusion | flops 805339136 | bytes 3276804 | tf_op jit(solution)/shard_map/dot_general | solution.py:85
  112.8 3.4 convolution_multiply_fusion.17
  116.2 3.4 convolution_multiply_fusion.16
  119.7 3.6 convolution_multiply_fusion.15
  123.3 0.8 pad_maximum_fusion
  124.1 13.2 %all-reduce.5.cloned.1.call-done = f32[256,256]{1,0:T(8,128)} async-done(((f32[256,256]{1,0:T(8,128)}), f32[256,256]{1,0:T(8,128)}) %all-reduce.5.cloned.1.call-update) | async-done | bytes 262160 | tf_op jit(solution)/shard_map/psum | solution.py:77
  137.4 221.3 %all-reduce.9.cloned.1.call-done = (f32[256,256]{1,0:T(8,128)}, f32[256,512]{1,0:T(8,128)}) async-done(((f32[256,256]{1,0:T(8,128)}, f32[256,512]{1,0:T(8,128)}), (f32[256,256]{1,0:T(8,128)}, f32[256,512]{1,0:T(8,128)})) %all-reduce.9.cloned.1.call-update) | async-done | bytes 786448 | tf_op jit(solution)/shard_map/psum | solution.py:77
  358.7 1.6 multiply_reduce_fusion.1
  361.0 1.3 select_subtract_fusion.13
  362.3 1.3 fusion.31
  363.9 0.4 select_subtract_fusion.12
  365.1 0.4 select_subtract_fusion.11
  366.3 0.4 select_subtract_fusion.10
  367.4 0.4 select_subtract_fusion.9
  369.8 0.4 select_subtract_fusion.7
  370.6 0.7 copy-done.12
  371.3 0.6 fusion.59
  371.9 1.3 fusion.60
  373.5 1.6 gather_fusion.1
  375.1 29.8 %all-reduce.7.cloned.1.call-done = f32[256,256]{1,0:T(8,128)} async-done(((f32[256,256]{1,0:T(8,128)}), f32[256,256]{1,0:T(8,128)}) %all-reduce.7.cloned.1.call-update) | async-done | bytes 262160 | tf_op jit(solution)/shard_map/psum | solution.py:105
  405.0 1.6 multiply_reduce_fusion
  407.3 1.3 select_subtract_fusion.6
  408.8 1.3 fusion.32
  410.2 0.4 select_subtract_fusion.5
  413.7 0.4 select_subtract_fusion.2
  414.8 0.4 select_subtract_fusion.1
  415.2 1.1 fusion.70
  416.7 1.3 select_subtract_fusion
  418.5 1.4 fusion.28
  419.9 1.8 fusion.72
  421.8 1.0 copy-done.9
  422.7 1.5 fusion.8
  424.2 2.0 div.43
  426.3 15.3 %reduce-scatter.7.cloned.1.call-done = f32[1024,1]{1,0:T(8,128)} async-done(((f32[2048,1]{1,0:T(8,128)}), f32[1024,1]{1,0:T(8,128)}) %reduce-scatter.7.cloned.1.call-update) | async-done | bytes 4112
  441.6 1.8 copy.11
  (89 shorter events, 11.5 us)
Async XLA Ops:
  7.2 3.1 copy-start
  10.3 18.6 %copy-start.18 = (f32[3]{0:T(128)S(1)}, f32[3]{0:T(128)}, u32[]{:S(2)}) copy-start(f32[3]{0:T(128)} %param.14) | copy-start | bytes 40
  10.3 22.6 %copy-start.19 = (s32[3]{0:T(128)S(1)}, s32[3]{0:T(128)}, u32[]{:S(2)}) copy-start(s32[3]{0:T(128)} %param.13) | copy-start | bytes 40
  10.3 28.1 %copy-start.17 = (s32[1024]{0:T(1024)S(1)}, s32[1024]{0:T(1024)}, u32[]{:S(2)}) copy-start(s32[1024]{0:T(1024)} %param.15) | copy-start | bytes 12292
  12.5 43.6 %all-to-all-start = ((f32[128,16,128]{2,1,0:T(8,128)}), f32[128,16,128]{2,1,0:T(8,128)S(1)}, u32[]{:S(2)}, u32[]{:S(2)}) async-start(f32[128,16,128]{2,1,0:T(8,128)} %bitcast.1), calls=%async_computation | async-start | bytes 2097152 | tf_op jit(solution)/shard_map/all_to_all | solution.py:64
  28.8 54.8 %reduce-scatter.5.cloned.1.call-start = ((), (), s32[]{:S(2)}) async-start(), calls=%async_computation.3 | async-start | bytes 3145728 | tf_op jit(solution)/shard_map/reduce_scatter | solution.py:70
  56.1 7.7 %copy-start.2 = (f32[128,16,128]{2,1,0:T(8,128)}, f32[128,16,128]{2,1,0:T(8,128)S(1)}, u32[]{:S(2)}) copy-start(f32[128,16,128]{2,1,0:T(8,128)S(1)} %all-to-all-done) | copy-start | bytes 3145732
  57.7 1.0 copy-start.3
  60.7 1.0 copy-start.5
  61.7 1.8 copy-start.20
  63.7 1.0 copy-start.7
  63.7 1.6 copy-start.13
  63.8 1.9 copy-start.14
  63.8 1.9 copy-start.16
  70.6 32.2 %all-gather.2.cloned.1.call-start = ((), (), s32[]{:S(2)}) async-start(), calls=%async_computation.4 | async-start | bytes 3145728 | tf_op jit(solution)/shard_map/all_gather | solution.py:71
  83.7 53.6 %all-reduce.5.cloned.1.call-start = ((), (), s32[]{:S(2)}) async-start(), calls=%async_computation.5 | async-start | bytes 524288 | tf_op jit(solution)/shard_map/psum | solution.py:77
  106.8 5.9 %copy-start.1 = (f32[2048,256]{1,0:T(8,128)S(1)}, f32[2048,256]{1,0:T(8,128)}, u32[]{:S(2)}) copy-start(f32[2048,256]{1,0:T(8,128)} %all-gather.2.cloned.1.call-done) | copy-start | bytes 6291460
  106.8 251.9 %all-reduce.9.cloned.1.call-start = ((), (), s32[]{:S(2)}) async-start(), calls=%async_computation.8 | async-start | bytes 1572864 | tf_op jit(solution)/shard_map/psum | solution.py:77
  107.4 5.4 %copy-start.8 = (f32[128,16,128]{2,1,0:T(8,128)S(1)}, f32[128,16,128]{2,1,0:T(8,128)}, u32[]{:S(2)}) copy-start(f32[128,16,128]{2,1,0:T(8,128)} %copy-done.7) | copy-start | bytes 3145732
  112.7 3.5 copy-start.4
  116.2 3.5 copy-start.6
  119.7 17.7 %copy-start.21 = (s32[1,32]{1,0:T(1,128)S(1)}, s32[1,32]{1,0:T(1,128)}, u32[]{:S(2)}) copy-start(s32[1,32]{1,0:T(1,128)} %param.17) | copy-start | bytes 388
  137.4 267.6 %all-reduce.7.cloned.1.call-start = ((), (), s32[]{:S(2)}) async-start(), calls=%async_computation.6 | async-start | bytes 524288 | tf_op jit(solution)/shard_map/psum | solution.py:105
  368.6 2.7 copy-start.15
  369.8 3.8 copy-start.11
  370.6 0.7 copy-start.12
  373.2 68.3 %reduce-scatter.7.cloned.1.call-start = ((), (), s32[]{:S(2)}) async-start(), calls=%async_computation.7 | async-start | bytes 1572864
  418.5 4.3 copy-start.10
  421.7 1.0 copy-start.9
Sparse Core Ops, SparseCore 0:
  70.7 12.9 reduce-scatter.4
  85.6 17.0 all-gather.1
  107.0 30.3 all-reduce.4
  143.3 215.3 all-reduce.8
  373.4 31.5 all-reduce.6
  426.4 15.1 reduce-scatter.6
